TPU v7x, 512 devices: a whole 4x4x16 slice. The times are simulated.
512 devices in a mesh: rep: 16 (over x, z_lo), mp: 32 (over z_hi, y, core).
Axes of the slice: x: 4, y: 4, z: 16 (z_hi: 4, z_lo: 4; z = z_hi * 4 + z_lo), core: 2. Of those that a mesh axis runs over, the one named last changes fastest.
Arguments:
- dense_feats: bfloat16 [65536, 13], P(('rep', 'mp')), may hold values from -6 to 6
- bag_counts: int32 [65536, 32, 64], P('rep', 'mp'), may hold values from 0 to 2
- emb_rows: bfloat16 [32, 64, 256], P('mp'), may hold values from -0.625 to 0.625
- v_emb: bfloat16 [8192, 256], P('mp'), may hold values from -0.0625 to 0.0625
- u_emb: bfloat16 [256, 8192], P(None, 'mp'), may hold values from -0.375 to 0.375
- b_emb: bfloat16 [8192], P('mp'), may hold values from -3 to 3
- v_bot: bfloat16 [256, 256], replicated, may hold values from -0.375 to 0.375
- u_bot: bfloat16 [256, 256], replicated, may hold values from -0.375 to 0.375
- b_bot: bfloat16 [256], replicated, may hold values from -3 to 3
- w_first: bfloat16 [13, 1024], replicated, may hold values from -1.75 to 1.75
- b_first: bfloat16 [1024], replicated, may hold values from -3 to 3
- w_second: bfloat16 [1024, 256], replicated, may hold values from -0.1875 to 0.1875
- b_second: bfloat16 [256], replicated, may hold values from -3 to 3
- cot_cross: bfloat16 [65536, 8192], P(('rep', 'mp')), may hold values from -24 to 24
- cot_bottom: bfloat16 [65536, 256], P(('rep', 'mp')), may hold values from -6 to 6
Outputs:
- cross_emb: bfloat16 [65536, 8192], P(('rep', 'mp'))
- cross_bot: bfloat16 [65536, 256], P(('rep', 'mp'))
- grad_table: bfloat16 [32, 64, 256], P('mp')
- grad_v_emb: bfloat16 [8192, 256], P('mp')
- grad_u_emb: bfloat16 [256, 8192], P(None, 'mp')
- grad_b_emb: bfloat16 [8192], P('mp')
- grad_v_bot: bfloat16 [256, 256], replicated
- grad_u_bot: bfloat16 [256, 256], replicated
- grad_b_bot: bfloat16 [256], replicated
- grad_w_first: bfloat16 [13, 1024], replicated
- grad_b_first: bfloat16 [1024], replicated
- grad_w_second: bfloat16 [1024, 256], replicated
- grad_b_second: bfloat16 [256], replicated
Inputs may be any that keep to these rules, and one draw needn't show every extreme that they name: bag_counts[s, t, j] is how often row j of table t occurs in the bag of sample s.
All inputs are finite; a program needn't handle non-finite values.
Results may differ from a plain program's by a relative error of at most 0.029.
Values may be sent and summed in bfloat16 or wider, within the bound.
A program may use at most 64 MiB of HBM per device.

v0:
```python
import math
import jax
import jax.numpy as jnp
from jax import lax
from jax.sharding import PartitionSpec as P


def silu_slope(inputs):
    gate_value = jax.nn.sigmoid(inputs)
    return gate_value * (1.0 + inputs * (1.0 - gate_value))


def contract_rows(left_side, right_side):
    return lax.dot_general(
        left_side, right_side, (((0,), (0,)), ((), ())), preferred_element_type=jnp.float32
    )


def contract_cols(left_side, right_side):
    return lax.dot_general(
        left_side, right_side, (((1,), (1,)), ((), ())), preferred_element_type=jnp.float32
    )


def local(
    dense_feats,
    bag_counts,
    emb_rows,
    v_emb,
    u_emb,
    b_emb,
    v_bot,
    u_bot,
    b_bot,
    w_first,
    b_first,
    w_second,
    b_second,
    cot_cross,
    cot_bottom,
):
    group_size = lax.axis_size("mp")
    own_rows = dense_feats.shape[0]
    first_row = lax.axis_index("mp") * own_rows
    grad_scale = 1.0 / math.sqrt(own_rows * group_size * lax.axis_size("rep"))
    counts = bag_counts[:, 0, :].astype(jnp.bfloat16)
    pooled = jnp.dot(counts, emb_rows[0], preferred_element_type=jnp.float32).astype(jnp.bfloat16)
    partial_value = jnp.dot(pooled, v_emb, preferred_element_type=jnp.float32)
    first_pre = jnp.dot(dense_feats, w_first, preferred_element_type=jnp.float32) + b_first.astype(
        jnp.float32
    )
    first_act = jax.nn.silu(first_pre).astype(jnp.bfloat16)
    second_pre = jnp.dot(first_act, w_second, preferred_element_type=jnp.float32) + b_second.astype(
        jnp.float32
    )
    bottom = jax.nn.silu(second_pre).astype(jnp.bfloat16)
    own_part = lax.dynamic_slice_in_dim(partial_value, first_row, own_rows, 0) + jnp.dot(
        bottom, v_bot, preferred_element_type=jnp.float32
    )
    partial_value = lax.dynamic_update_slice_in_dim(partial_value, own_part, first_row, 0)
    low_rank = lax.psum(partial_value.astype(jnp.bfloat16), "mp")
    lift_emb = jnp.dot(low_rank, u_emb, preferred_element_type=jnp.float32) + b_emb.astype(
        jnp.float32
    )
    pooled_full = pooled.astype(jnp.float32)
    cross_local = (pooled_full * (lift_emb + 1.0)).astype(jnp.bfloat16)
    cross_emb = lax.all_to_all(cross_local, "mp", split_axis=0, concat_axis=1, tiled=True)
    own_low = lax.dynamic_slice_in_dim(low_rank, first_row, own_rows, 0)
    lift_bottom = jnp.dot(own_low, u_bot, preferred_element_type=jnp.float32) + b_bot.astype(
        jnp.float32
    )
    bottom_full = bottom.astype(jnp.float32)
    cross_bot = (bottom_full * (lift_bottom + 1.0)).astype(jnp.bfloat16)
    cot_rows = lax.all_to_all(cot_cross, "mp", split_axis=1, concat_axis=0, tiled=True).astype(
        jnp.float32
    )
    d_lift = cot_rows * pooled_full
    d_lift_round = d_lift.astype(jnp.bfloat16)
    own_back = lax.psum_scatter(
        contract_cols(d_lift_round, u_emb).astype(jnp.bfloat16),
        "mp",
        scatter_dimension=0,
        tiled=True,
    ).astype(jnp.float32)
    cot_low = cot_bottom.astype(jnp.float32)
    d_bottom_lift = cot_low * bottom_full
    d_bottom_round = d_bottom_lift.astype(jnp.bfloat16)
    own_d_low = (own_back + contract_cols(d_bottom_round, u_bot)).astype(jnp.bfloat16)
    d_low = lax.all_gather(own_d_low, "mp", axis=0, tiled=True)
    d_pooled = (cot_rows * (lift_emb + 1.0) + contract_cols(d_low, v_emb)).astype(jnp.bfloat16)
    grad_table = grad_scale * contract_rows(counts, d_pooled)
    grad_v = grad_scale * contract_rows(pooled, d_low)
    grad_u = grad_scale * contract_rows(low_rank, d_lift_round)
    grad_b = grad_scale * jnp.sum(d_lift, axis=0)
    d_bottom = cot_low * (lift_bottom + 1.0) + contract_cols(own_d_low, v_bot)
    grad_vb = grad_scale * contract_rows(bottom, own_d_low)
    grad_ub = grad_scale * contract_rows(own_low, d_bottom_round)
    grad_bb = grad_scale * jnp.sum(d_bottom_lift, axis=0)
    d_second = d_bottom * silu_slope(second_pre)
    d_second_round = d_second.astype(jnp.bfloat16)
    grad_ws = grad_scale * contract_rows(first_act, d_second_round)
    grad_bs = grad_scale * jnp.sum(d_second, axis=0)
    d_first = contract_cols(d_second_round, w_second) * silu_slope(first_pre)
    d_first_round = d_first.astype(jnp.bfloat16)
    grad_wf = grad_scale * contract_rows(dense_feats, d_first_round)
    grad_bf = grad_scale * jnp.sum(d_first, axis=0)
    dense_sums = lax.psum(
        (grad_wf, grad_bf, grad_ws, grad_bs, grad_vb, grad_ub, grad_bb), ("rep", "mp")
    )
    table_sums = (
        lax.psum(grad_table.astype(jnp.bfloat16), "rep").astype(jnp.float32),
        lax.psum(grad_v.astype(jnp.bfloat16), "rep").astype(jnp.float32),
        lax.psum(grad_u.astype(jnp.bfloat16), "rep").astype(jnp.float32),
        lax.psum(grad_b.astype(jnp.bfloat16), "rep").astype(jnp.float32),
    )
    return (
        cross_emb,
        cross_bot,
        table_sums[0][None].astype(jnp.bfloat16),
        table_sums[1].astype(jnp.bfloat16),
        table_sums[2].astype(jnp.bfloat16),
        table_sums[3].astype(jnp.bfloat16),
        dense_sums[4].astype(jnp.bfloat16),
        dense_sums[5].astype(jnp.bfloat16),
        dense_sums[6].astype(jnp.bfloat16),
        dense_sums[0].astype(jnp.bfloat16),
        dense_sums[1].astype(jnp.bfloat16),
        dense_sums[2].astype(jnp.bfloat16),
        dense_sums[3].astype(jnp.bfloat16),
    )


def solution(mesh):
    return jax.shard_map(
        local,
        mesh=mesh,
        in_specs=(
            P(("rep", "mp"), None),
            P("rep", "mp", None),
            P("mp", None, None),
            P("mp", None),
            P(None, "mp"),
            P("mp"),
            P(),
            P(),
            P(),
            P(),
            P(),
            P(),
            P(),
            P(("rep", "mp"), None),
            P(("rep", "mp"), None),
        ),
        out_specs=(
            P(("rep", "mp"), None),
            P(("rep", "mp"), None),
            P("mp", None, None),
            P("mp", None),
            P(None, "mp"),
            P("mp"),
            P(),
            P(),
            P(),
            P(),
            P(),
            P(),
            P(),
        ),
        check_vma=False,
    )
```

profile of v0, /device:TPU:8, one launch (start us, length us, event | category | flops | bytes accessed | tf_op | source)
XLA Modules:
  0.0 923.8 jit_solution(9754976400988497330)
XLA Ops:
  7.2 3.2 copy.33
  10.4 18.5 %all-to-all-start.1 = ((bf16[128,32,256]{2,0,1:T(8,128)(2,1)}), bf16[128,32,256]{2,0,1:T(8,128)(2,1)}, u32[]{:S(2)}, u32[]{:S(2)}) async-start(bf16[128,32,256]{2,0,1:T(8,128)(2,1)} %bitcast.58), calls=%async_computation.1 | async-start | bytes 4194304 | tf_op jit(solution)/shard_map/all_to_all | solution.py:74
  29.1 0.3 convolution_add_fusion.2
  29.4 0.8 copy-done.5
  30.2 1.0 fusion.22
  31.1 2.0 convolution_convert_fusion.1
  33.1 0.7 fusion.35
  33.9 0.2 copy-done.9
  34.2 1.5 convert_element_type.134
  35.8 0.6 copy-done.16
  36.4 399.7 %all-reduce.7.cloned.1.call-done = bf16[4096,256]{1,0:T(8,128)(2,1)} async-done(((bf16[4096,256]{1,0:T(8,128)(2,1)}), bf16[4096,256]{1,0:T(8,128)(2,1)}) %all-reduce.7.cloned.1.call-update) | async-done | bytes 2097168 | tf_op jit(solution)/shard_map/psum | solution.py:61
  436.1 6.4 bitcast_multiply_fusion
  442.6 1.3 copy-done.1
  443.9 2.1 convolution_convert_fusion
  446.1 21.6 %all-to-all-start = ((bf16[32,128,256]{2,1,0:T(8,128)(2,1)}), bf16[32,128,256]{2,1,0:T(8,128)(2,1)}, u32[]{:S(2)}, u32[]{:S(2)}) async-start(bf16[32,128,256]{2,1,0:T(8,128)(2,1)} %bitcast.59), calls=%async_computation | async-start | bytes 4194304 | tf_op jit(solution)/shard_map/all_to_all | solution.py:67
  467.7 151.9 %reduce-scatter.2.cloned.1.call-done = bf16[128,256]{1,0:T(8,128)(2,1)} async-done(((bf16[4096,256]{1,0:T(8,128)(2,1)}), bf16[128,256]{1,0:T(8,128)(2,1)}) %reduce-scatter.2.cloned.1.call-update) | async-done | bytes 65552 | tf_op jit(solution)/shard_map/reduce_scatter | solution.py:79
  619.7 1.7 fusion.11
  621.4 1.1 convolution_multiply_fusion.2
  622.5 1.6 fusion.21
  624.2 3.7 fusion.7
  627.9 0.2 convolution_multiply_fusion.3
  628.1 0.2 fusion.34
  628.4 0.4 fusion.33
  628.9 1.4 convolution_multiply_fusion
  630.3 114.5 %all-reduce.10 = (bf16[256,256]{1,0:T(8,128)(2,1)}, bf16[256,256]{1,0:T(8,128)(2,1)}, bf16[256]{0:T(256)(128)(2,1)}, bf16[13,1024]{1,0:T(8,128)(2,1)}, bf16[1024...) all-reduce(f32[256,256]{1,0:T(8,128)S(1)} %convolution_multiply_fus, ...), channel_id=1, replica_groups=mesh['rep'=16,'mp'=32] {'rep','mp'}, use_global_device_ids=true, to_apply=%region_7.8 | all-reduce | flops 408064 | bytes 2448384 | tf_op jit(solution)/shard_map/psum | solution.py:107
  744.8 3.0 fusion.6
  747.8 4.5 fusion.15
  752.3 78.6 %all-reduce.1 = (bf16[1,64,256]{2,1,0:T(8,128)(2,1)}, bf16[256]{0:T(256)(128)(2,1)}) all-reduce(bf16[1,64,256]{2,1,0:T(8,128)(2,1)S(1)} %fusion.15, bf16[256]{0:T(256)(128)(2,1)S(1)} %multiply_convert_fusion.2), channel_id=1, replica_groups=mesh['rep'=16,'mp'=32] {'rep'}, use_global_device_ids=true, to_apply=%region_2.3 | all-reduce | flops 16640 | bytes 66560 | tf_op jit(solution)/shard_map/psum | solution.py:111
  830.9 3.1 copy.31
  834.0 80.1 %all-reduce.9.cloned.1.call-done = (bf16[256,256]{1,0:T(8,128)(2,1)}, bf16[256,256]{1,0:T(8,128)(2,1)}) async-done(((bf16[256,256]{1,0:T(8,128)(2,1)}, bf16[256,256]{1,0:T(8,128)(2,1)}), (bf16[256,256]{1,0:T(8,128)(2,1)}, bf16[256,256]{1,0:T(8,128)(2,1)})) %all-reduce.9.cloned.1.call-update) | async-done | bytes 262160 | tf_op jit(solution)/shard_map/psum | solution.py:112
  914.1 1.6 copy.52
  915.7 1.6 copy.53
  (55 shorter events, 0.7 us)
Async XLA Ops:
  7.2 23.0 %copy-start = (bf16[1024,256]{1,0:T(8,128)(2,1)S(1)}, bf16[1024,256]{1,0:T(8,128)(2,1)}, u32[]{:S(2)}) copy-start(bf16[1024,256]{1,0:T(8,128)(2,1)} %param.26) | copy-start | bytes 1572868
  10.4 18.6 %copy-start.15 = (bf16[256]{0:T(256)(128)(2,1)S(1)}, bf16[256]{0:T(256)(128)(2,1)}, u32[]{:S(2)}) copy-start(bf16[256]{0:T(256)(128)(2,1)} %param.27) | copy-start | bytes 1540
  10.4 18.6 %copy-start.14 = (bf16[1024]{0:T(1024)(128)(2,1)S(1)}, bf16[1024]{0:T(1024)(128)(2,1)}, u32[]{:S(2)}) copy-start(bf16[1024]{0:T(1024)(128)(2,1)} %param.25) | copy-start | bytes 6148
  10.4 18.7 %copy-start.12 = (bf16[13,1024]{1,0:T(8,128)(2,1)S(1)}, bf16[13,1024]{1,0:T(8,128)(2,1)}, u32[]{:S(2)}) copy-start(bf16[13,1024]{1,0:T(8,128)(2,1)} %param.24) | copy-start | bytes 79876
  10.4 18.7 %copy-start.13 = (bf16[128,13]{0,1:T(8,128)(2,1)S(1)}, bf16[128,13]{0,1:T(8,128)(2,1)}, u32[]{:S(2)}) copy-start(bf16[128,13]{0,1:T(8,128)(2,1)} %param.15) | copy-start | bytes 9988
  10.4 19.7 %copy-start.8 = (bf16[128,256]{1,0:T(8,128)(2,1)S(1)}, bf16[128,256]{1,0:T(8,128)(2,1)}, u32[]{:S(2)}) copy-start(bf16[128,256]{1,0:T(8,128)(2,1)} %param.29) | copy-start | bytes 196612
  10.4 425.7 %all-to-all-start.1 = ((bf16[128,32,256]{2,0,1:T(8,128)(2,1)}), bf16[128,32,256]{2,0,1:T(8,128)(2,1)}, u32[]{:S(2)}, u32[]{:S(2)}) async-start(bf16[128,32,256]{2,0,1:T(8,128)(2,1)} %bitcast.58), calls=%async_computation.1 | async-start | bytes 4194304 | tf_op jit(solution)/shard_map/all_to_all | solution.py:74
  29.0 2.1 copy-start.11
  29.0 407.2 %all-reduce.7.cloned.1.call-start = ((), (), s32[]{:S(2)}) async-start(), calls=%async_computation.3 | async-start | bytes 4194304 | tf_op jit(solution)/shard_map/psum | solution.py:61
  29.4 0.8 copy-start.5
  31.1 2.0 copy-start.4
  33.1 0.9 copy-start.9
  35.8 0.7 copy-start.16
  35.8 400.4 %copy-start.3 = (bf16[256,256]{1,0:T(8,128)(2,1)S(1)}, bf16[256,256]{1,0:T(8,128)(2,1)}, u32[]{:S(2)}) copy-start(bf16[256,256]{1,0:T(8,128)(2,1)} %param.19) | copy-start | bytes 393220
  35.8 583.9 %reduce-scatter.2.cloned.1.call-start = ((), (), s32[]{:S(2)}) async-start(), calls=%async_computation.4 | async-start | bytes 2162688 | tf_op jit(solution)/shard_map/reduce_scatter | solution.py:79
  442.6 1.3 copy-start.1
  446.0 173.6 %copy-start.7 = (bf16[256,256]{1,0:T(8,128)(2,1)S(1)}, bf16[256,256]{1,0:T(8,128)(2,1)}, u32[]{:S(2)}) copy-start(bf16[256,256]{1,0:T(8,128)(2,1)} %param.22) | copy-start | bytes 393220
  446.1 175.3 %copy-start.17 = (bf16[256]{0:T(256)(128)(2,1)S(1)}, bf16[256]{0:T(256)(128)(2,1)}, u32[]{:S(2)}) copy-start(bf16[256]{0:T(256)(128)(2,1)} %param.23) | copy-start | bytes 1540
  446.1 384.9 %all-to-all-start = ((bf16[32,128,256]{2,1,0:T(8,128)(2,1)}), bf16[32,128,256]{2,1,0:T(8,128)(2,1)}, u32[]{:S(2)}, u32[]{:S(2)}) async-start(bf16[32,128,256]{2,1,0:T(8,128)(2,1)} %bitcast.59), calls=%async_computation | async-start | bytes 4194304 | tf_op jit(solution)/shard_map/all_to_all | solution.py:67
  467.7 277.1 %all-gather.2.cloned.1.call-start = ((), (), s32[]{:S(2)}) async-start(), calls=%async_computation.5 | async-start | bytes 2162688 | tf_op jit(solution)/shard_map/all_gather | solution.py:89
  621.4 292.8 %all-reduce.9.cloned.1.call-start = ((), (), s32[]{:S(2)}) async-start(), calls=%async_computation.6 | async-start | bytes 524288 | tf_op jit(solution)/shard_map/psum | solution.py:112
  624.2 3.7 copy-start.2
  624.2 4.0 copy-start.10
  624.2 4.0 copy-start.18
  624.2 4.2 copy-start.6
Sparse Core Ops, SparseCore 0:
  35.9 400.1 all-reduce.6
  446.2 173.4 reduce-scatter.1
  623.8 74.0 all-gather.1
  747.9 166.1 all-reduce.8
where the time goes:
time: 924 us
  waiting for transfers between devices  632 us (68%)
  blocking collectives  193 us (21%)
  starting transfers between devices  40.3 us (4%)
  matrix products  30.5 us (3%)
  between operations  14.1 us (2%)
  local copies, waits for them, and re-layouts  12.5 us (1%)
    psum x1, waiting for transfers between devices, local(): low_rank = lax.psum(partial_value.astype(jnp.bfloat16), 'mp')  400 us
    reduce_scatter x1, waiting for transfers between devices, local(): lax.psum_scatter(contract_cols(d_lift_round, u_emb).astype(jnp.bfloat16),...  152 us
    psum x1, blocking collectives, local(): lax.psum((grad_wf, grad_bf, grad_ws, grad_bs, grad_vb, grad_ub, grad_bb),...  115 us
    psum x1, waiting for transfers between devices, local(): lax.psum(grad_v.astype(jnp.bfloat16), 'rep').astype(jnp.float32)  80.1 us
    psum x1, blocking collectives, local(): lax.psum(grad_table.astype(jnp.bfloat16), 'rep').astype(jnp.float32)  78.6 us
    all_to_all x1, starting transfers between devices, local(): lax.all_to_all(cross_local, 'mp', split_axis=0, concat_axis=1, tiled=True)  21.6 us
    all_to_all x1, starting transfers between devices, local(): lax.all_to_all(cot_cross, 'mp', split_axis=1, concat_axis=0, tiled=True)  18.5 us
  transfers between devices with their start and end apart: 6, of which 3 were waited for; matrix products, arithmetic and copies ran while one was open for 3% of the time, Pallas kernels for 0%

commit v1 on v0

--- a/solution.py
+++ b/solution.py
@@ -109,7 +109,7 @@
     )
     table_sums = (
         lax.psum(grad_table.astype(jnp.bfloat16), "rep").astype(jnp.float32),
-        lax.psum(grad_v.astype(jnp.bfloat16), "rep").astype(jnp.float32),
+        jnp.sum(lax.all_gather(grad_v.astype(jnp.bfloat16), "rep"), axis=0).astype(jnp.float32),
         lax.psum(grad_u.astype(jnp.bfloat16), "rep").astype(jnp.float32),
         lax.psum(grad_b.astype(jnp.bfloat16), "rep").astype(jnp.float32),
     )

time: 924 us -> 1010 us (1.093)
  waiting for transfers between devices: 632 us -> 728 us
  starting transfers between devices: 40.3 us -> 28.3 us
    all_gather x1, waiting for transfers between devices: 0.01 us -> 148 us  [local(): d_low = lax.all_gather(own_d_low, 'mp', axis=0, tiled=True)]
    psum x1, waiting for transfers between devices: 80.1 us -> 51.2 us  [local(): lax.psum(grad_u.astype(jnp.bfloat16), 'rep').astype(jnp.float32)]
    reduce_scatter x1, waiting for transfers between devices: 152 us -> 128 us  [local(): lax.psum_scatter(contract_cols(d_lift_round, u_emb).astype(jnp.bfloat16),...]
    all_to_all x1, starting transfers between devices: 21.6 us -> 9.54 us  [local(): lax.all_to_all(cross_local, 'mp', split_axis=0, concat_axis=1, tiled=True)]
  transfers between devices with their start and end apart: 6 -> 7, of which waited for: 3 -> 4; matrix products, arithmetic and copies ran while one was open for 3% -> 3% of each run, Pallas kernels for 0% -> 0%
where the time goes in v1:
time: 1010 us; the launch traced here: 1000 us
  waiting for transfers between devices  728 us (72%)
  blocking collectives  189 us (19%)
  matrix products  29.2 us (3%)
  starting transfers between devices  28.3 us (3%)
  between operations  14.1 us (1%)
  local copies, waits for them, and re-layouts  11.2 us (1%)
    psum x1, waiting for transfers between devices, local(): low_rank = lax.psum(partial_value.astype(jnp.bfloat16), 'mp')  401 us
    all_gather x1, waiting for transfers between devices, local(): d_low = lax.all_gather(own_d_low, 'mp', axis=0, tiled=True)  148 us
    reduce_scatter x1, waiting for transfers between devices, local(): lax.psum_scatter(contract_cols(d_lift_round, u_emb).astype(jnp.bfloat16),...  128 us
    psum x1, blocking collectives, local(): lax.psum((grad_wf, grad_bf, grad_ws, grad_bs, grad_vb, grad_ub, grad_bb),...  111 us
    psum x1, blocking collectives, local(): lax.psum(grad_table.astype(jnp.bfloat16), 'rep').astype(jnp.float32)  77.8 us
    psum x1, waiting for transfers between devices, local(): lax.psum(grad_u.astype(jnp.bfloat16), 'rep').astype(jnp.float32)  51.2 us
  transfers between devices with their start and end apart: 7, of which 4 were waited for; matrix products, arithmetic and copies ran while one was open for 3% of the time, Pallas kernels for 0%

profile of v1, /device:TPU:8, one launch (start us, length us, event | category | flops | bytes accessed | tf_op | source)
XLA Modules:
  0.0 1004.4 jit_solution(12979561957651060080)
XLA Ops:
  7.2 3.2 copy.33
  10.4 18.5 %all-to-all-start.1 = ((bf16[128,32,256]{2,0,1:T(8,128)(2,1)}), bf16[128,32,256]{2,0,1:T(8,128)(2,1)}, u32[]{:S(2)}, u32[]{:S(2)}) async-start(bf16[128,32,256]{2,0,1:T(8,128)(2,1)} %bitcast.59), calls=%async_computation.1 | async-start | bytes 4194304 | tf_op jit(solution)/shard_map/all_to_all | solution.py:74
  29.1 0.2 convolution_add_fusion.2
  29.4 0.8 copy-done.6
  30.2 1.0 fusion.22
  31.1 2.0 convolution_convert_fusion.1
  33.1 0.7 fusion.35
  34.2 1.5 convert_element_type.136
  35.8 0.6 copy-done.17
  36.4 400.6 %all-reduce.6.cloned.1.call-done = bf16[4096,256]{1,0:T(8,128)(2,1)} async-done(((bf16[4096,256]{1,0:T(8,128)(2,1)}), bf16[4096,256]{1,0:T(8,128)(2,1)}) %all-reduce.6.cloned.1.call-update) | async-done | bytes 2097168 | tf_op jit(solution)/shard_map/psum | solution.py:61
  437.0 6.4 bitcast_multiply_fusion
  443.5 1.4 copy-done.1
  444.8 2.1 convolution_convert_fusion
  447.0 128.1 %reduce-scatter.2.cloned.1.call-done = bf16[128,256]{1,0:T(8,128)(2,1)} async-done(((bf16[4096,256]{1,0:T(8,128)(2,1)}), bf16[128,256]{1,0:T(8,128)(2,1)}) %reduce-scatter.2.cloned.1.call-update) | async-done | bytes 65552 | tf_op jit(solution)/shard_map/reduce_scatter | solution.py:79
  575.1 1.7 fusion.11
  576.8 9.5 all-to-all-start
  586.4 148.3 %all-gather.4.cloned.1.call-done = bf16[4096,256]{1,0:T(8,128)(2,1)} async-done(((bf16[128,256]{1,0:T(8,128)(2,1)}), bf16[4096,256]{1,0:T(8,128)(2,1)}) %all-gather.4.cloned.1.call-update) | async-done | bytes 2097168 | tf_op jit(solution)/shard_map/all_gather | solution.py:89
  734.7 3.0 fusion.6
  737.9 1.1 convolution_multiply_fusion.2
  738.9 1.6 fusion.21
  740.6 3.7 fusion.7
  744.6 0.2 fusion.34
  744.8 0.4 fusion.33
  745.3 0.3 copy-done.8
  745.6 0.4 convolution_multiply_fusion
  746.0 111.5 %all-reduce.9 = (bf16[256,256]{1,0:T(8,128)(2,1)}, bf16[256,256]{1,0:T(8,128)(2,1)}, bf16[256]{0:T(256)(128)(2,1)}, bf16[13,1024]{1,0:T(8,128)(2,1)}, bf16[1024]...) all-reduce(f32[256,256]{1,0:T(8,128)S(1)} %convolution_multiply_fus, ...), channel_id=1, replica_groups=mesh['rep'=16,'mp'=32] {'rep','mp'}, use_global_device_ids=true, to_apply=%region_7.8 | all-reduce | flops 408064 | bytes 2448384 | tf_op jit(solution)/shard_map/psum | solution.py:107
  857.5 4.1 fusion.15
  861.6 77.8 %all-reduce.1 = (bf16[1,64,256]{2,1,0:T(8,128)(2,1)}, bf16[256]{0:T(256)(128)(2,1)}) all-reduce(bf16[1,64,256]{2,1,0:T(8,128)(2,1)S(1)} %fusion.15, bf16[256]{0:T(256)(128)(2,1)S(1)} %multiply_convert_fusion.2), channel_id=1, replica_groups=mesh['rep'=16,'mp'=32] {'rep'}, use_global_device_ids=true, to_apply=%region_2.3 | all-reduce | flops 16640 | bytes 66560 | tf_op jit(solution)/shard_map/psum | solution.py:111
  939.4 3.1 copy.31
  942.5 2.6 reduce_sum.48
  945.1 51.2 %all-reduce.8.cloned.1.call-done = bf16[256,256]{1,0:T(8,128)(2,1)} async-done(((bf16[256,256]{1,0:T(8,128)(2,1)}), bf16[256,256]{1,0:T(8,128)(2,1)}) %all-reduce.8.cloned.1.call-update) | async-done | bytes 131088 | tf_op jit(solution)/shard_map/psum | solution.py:113
  996.3 1.6 copy.51
  (60 shorter events, 1.1 us)
Async XLA Ops:
  7.2 23.0 %copy-start = (bf16[1024,256]{1,0:T(8,128)(2,1)S(1)}, bf16[1024,256]{1,0:T(8,128)(2,1)}, u32[]{:S(2)}) copy-start(bf16[1024,256]{1,0:T(8,128)(2,1)} %param.26) | copy-start | bytes 1572868
  10.4 18.6 %copy-start.16 = (bf16[256]{0:T(256)(128)(2,1)S(1)}, bf16[256]{0:T(256)(128)(2,1)}, u32[]{:S(2)}) copy-start(bf16[256]{0:T(256)(128)(2,1)} %param.27) | copy-start | bytes 1540
  10.4 18.6 %copy-start.15 = (bf16[1024]{0:T(1024)(128)(2,1)S(1)}, bf16[1024]{0:T(1024)(128)(2,1)}, u32[]{:S(2)}) copy-start(bf16[1024]{0:T(1024)(128)(2,1)} %param.25) | copy-start | bytes 6148
  10.4 18.7 %copy-start.13 = (bf16[13,1024]{1,0:T(8,128)(2,1)S(1)}, bf16[13,1024]{1,0:T(8,128)(2,1)}, u32[]{:S(2)}) copy-start(bf16[13,1024]{1,0:T(8,128)(2,1)} %param.24) | copy-start | bytes 79876
  10.4 18.7 %copy-start.14 = (bf16[128,13]{0,1:T(8,128)(2,1)S(1)}, bf16[128,13]{0,1:T(8,128)(2,1)}, u32[]{:S(2)}) copy-start(bf16[128,13]{0,1:T(8,128)(2,1)} %param.15) | copy-start | bytes 9988
  10.4 19.7 %copy-start.10 = (bf16[128,256]{1,0:T(8,128)(2,1)S(1)}, bf16[128,256]{1,0:T(8,128)(2,1)}, u32[]{:S(2)}) copy-start(bf16[128,256]{1,0:T(8,128)(2,1)} %param.29) | copy-start | bytes 196612
  10.4 426.6 %all-to-all-start.1 = ((bf16[128,32,256]{2,0,1:T(8,128)(2,1)}), bf16[128,32,256]{2,0,1:T(8,128)(2,1)}, u32[]{:S(2)}, u32[]{:S(2)}) async-start(bf16[128,32,256]{2,0,1:T(8,128)(2,1)} %bitcast.59), calls=%async_computation.1 | async-start | bytes 4194304 | tf_op jit(solution)/shard_map/all_to_all | solution.py:74
  29.0 2.1 copy-start.12
  29.0 408.0 %all-reduce.6.cloned.1.call-start = ((), (), s32[]{:S(2)}) async-start(), calls=%async_computation.3 | async-start | bytes 4194304 | tf_op jit(solution)/shard_map/psum | solution.py:61
  29.4 0.8 copy-start.6
  31.1 2.0 copy-start.5
  33.1 0.9 copy-start.11
  35.7 0.7 copy-start.17
  35.7 401.3 %copy-start.4 = (bf16[256,256]{1,0:T(8,128)(2,1)S(1)}, bf16[256,256]{1,0:T(8,128)(2,1)}, u32[]{:S(2)}) copy-start(bf16[256,256]{1,0:T(8,128)(2,1)} %param.19) | copy-start | bytes 393220
  35.8 539.3 %reduce-scatter.2.cloned.1.call-start = ((), (), s32[]{:S(2)}) async-start(), calls=%async_computation.4 | async-start | bytes 2162688 | tf_op jit(solution)/shard_map/reduce_scatter | solution.py:79
  443.4 1.4 copy-start.1
  446.9 128.2 %copy-start.9 = (bf16[256,256]{1,0:T(8,128)(2,1)S(1)}, bf16[256,256]{1,0:T(8,128)(2,1)}, u32[]{:S(2)}) copy-start(bf16[256,256]{1,0:T(8,128)(2,1)} %param.22) | copy-start | bytes 393220
  446.9 287.8 %all-gather.4.cloned.1.call-start = ((), (), s32[]{:S(2)}) async-start(), calls=%async_computation.5 | async-start | bytes 2162688 | tf_op jit(solution)/shard_map/all_gather | solution.py:89
  576.8 362.6 %all-to-all-start = ((bf16[32,128,256]{2,1,0:T(8,128)(2,1)}), bf16[32,128,256]{2,1,0:T(8,128)(2,1)}, u32[]{:S(2)}, u32[]{:S(2)}) async-start(bf16[32,128,256]{2,1,0:T(8,128)(2,1)} %bitcast.60), calls=%async_computation | async-start | bytes 4194304 | tf_op jit(solution)/shard_map/all_to_all | solution.py:67
  586.3 151.5 %copy-start.18 = (bf16[256]{0:T(256)(128)(2,1)S(1)}, bf16[256]{0:T(256)(128)(2,1)}, u32[]{:S(2)}) copy-start(bf16[256]{0:T(256)(128)(2,1)} %param.23) | copy-start | bytes 1540
  586.3 356.2 %all-gather.6.cloned.1.call-start = ((), (), s32[]{:S(2)}) async-start(), calls=%async_computation.7 | async-start | bytes 2228224 | tf_op jit(solution)/shard_map/all_gather | solution.py:112
  737.8 258.6 %all-reduce.8.cloned.1.call-start = ((), (), s32[]{:S(2)}) async-start(), calls=%async_computation.6 | async-start | bytes 262144 | tf_op jit(solution)/shard_map/psum | solution.py:113
  740.6 3.8 copy-start.3
  740.6 4.0 copy-start.19
  740.6 4.2 copy-start.7
  744.6 1.0 copy-start.8
  745.6 111.9 %copy-start.2 = (s32[4096,1,64]{0,2,1:T(8,128)S(1)}, s32[4096,1,64]{0,2,1:T(8,128)}, u32[]{:S(2)}) copy-start(s32[4096,1,64]{0,2,1:T(8,128)} %param.16) | copy-start | bytes 3145732
Sparse Core Ops, SparseCore 0:
  35.9 401.0 all-reduce.5
  447.1 127.9 reduce-scatter.1
  579.3 155.4 all-gather.3
  737.9 87.6 all-gather.5
  828.6 167.7 all-reduce.7
